TPU v7x, 512 devices: a whole 4x8x8 slice. The times are simulated.
512 devices in a mesh: seq: 128 (over y, z, core), tp: 4 (over x).
Axes of the slice: x: 4, y: 8, z: 8, core: 2. Of those that a mesh axis runs over, the one named last changes fastest.
Arguments:
- queries: bfloat16 [16384, 4096], P('seq', 'tp'), may hold values from -12 to 12
- keys: bfloat16 [16384, 512], P('seq', 'tp'), may hold values from -12 to 12
- values: bfloat16 [16384, 512], P('seq', 'tp'), may hold values from -6 to 6
- sinks: float32 [64], P('tp'), may hold values from 0.5 to 4.5
- session_start: int32 [16384], P('seq'), may hold values from 0 to 16383, as said below
- residual: bfloat16 [16384, 2880], P('seq', 'tp'), may hold values from -40 to 40
- w_out: bfloat16 [4096, 2880], P('seq', 'tp'), may hold values from -0.09375 to 0.09375
- norm_gain: float32 [2880], P('tp'), may hold values from 0.1 to 1.9
- expert_ids: int32 [16384, 4], P('seq'), may hold values from 0 to 63, all different within a row; in each aligned block of 128 rows (0 to 127, 128 to 255, ...) at most 10 rows name the same one
- expert_gates: bfloat16 [16384, 4], P('seq'), may hold values from 0.099609375 to 0.59765625
- w_gate: bfloat16 [2880, 92160], P('tp', 'seq'), may hold values from -0.109375 to 0.109375
- w_up: bfloat16 [2880, 92160], P('tp', 'seq'), may hold values from -0.109375 to 0.109375
- w_down: bfloat16 [92160, 2880], P('seq', 'tp'), may hold values from -0.15625 to 0.15625
Outputs:
- layer_out: bfloat16 [16384, 2880], P('seq', 'tp')
Inputs may be any that keep to these rules, and one draw needn't show every extreme that they name: `expert_ids`: each row names 4 different experts. Within the rows of one seq index (aligned blocks of 128 rows) no expert is named by more than 10 rows, a bound that some block reaches. `session_start`: nondecreasing; each entry is the first position of its token's session, so session_start[i] <= i, with equality at a session's first token.
All inputs are finite; a program needn't handle non-finite values.
Results may differ from a plain program's by a relative error of at most 0.013.
Values may be sent and summed in bfloat16 or wider, within the bound.
No kernel may reach another device: no remote copies, remote signals or barrier semaphores. Data moves between devices by JAX's collectives and lax.ppermute only.
A program may use at most 64 MiB of HBM per device.

v0:
```python
import jax
import jax.numpy as jnp
from jax import lax
from jax.sharding import PartitionSpec as P

D = 2880
HEAD_SIZE = 64
WINDOW_SPAN = 128
TOP = 4
NEGATIVE = -1e30
EPSILON = 1e-05


def passed_along(block, axis, distance):
    devices = range(lax.axis_size(axis))
    route = [(i - distance, i) for i in devices if i - distance in devices]
    return lax.ppermute(block, axis, route)


def shards(
    queries,
    keys,
    values,
    sinks,
    session_start,
    residual,
    w_out,
    norm_gain,
    expert_ids,
    expert_gates,
    w_gate,
    w_up,
    w_down,
):
    tok_count = queries.shape[0]
    kv_heads = keys.shape[1] // HEAD_SIZE
    q_heads = queries.shape[1] // HEAD_SIZE
    query_groups = q_heads // kv_heads
    seq_index = lax.axis_index("seq")
    first_pos = seq_index * tok_count
    tail_rows = passed_along((keys, values), "seq", 1)
    all_keys = jnp.concatenate([tail_rows[0], keys], axis=0)
    all_values = jnp.concatenate([tail_rows[1], values], axis=0)
    key_count = all_keys.shape[0]
    query_pos = first_pos + jnp.arange(tok_count, dtype=jnp.int32)
    key_pos = first_pos - WINDOW_SPAN + jnp.arange(key_count, dtype=jnp.int32)
    distance = query_pos[:, None] - key_pos[None, :]
    allowed = (
        (distance >= 0) & (distance < WINDOW_SPAN) & (key_pos[None, :] >= session_start[:, None])
    )
    blocked_queries = queries.reshape(tok_count, kv_heads, query_groups, HEAD_SIZE)
    blocked_keys = all_keys.reshape(key_count, kv_heads, HEAD_SIZE)
    blocked_values = all_values.reshape(key_count, kv_heads, HEAD_SIZE)
    scores = jnp.einsum(
        "qhgd,khd->hgqk", blocked_queries, blocked_keys, preferred_element_type=jnp.float32
    ) * HEAD_SIZE ** (-0.5)
    scores = jnp.where(allowed[None, None], scores, NEGATIVE)
    sink_column = sinks.reshape(kv_heads, query_groups)[:, :, None, None]
    row_max = jnp.maximum(jnp.max(scores, axis=-1, keepdims=True), sink_column)
    numerator = jnp.exp(scores - row_max) * allowed[None, None].astype(jnp.float32)
    denominator = jnp.sum(numerator, axis=-1, keepdims=True) + jnp.exp(sink_column - row_max)
    weights = (numerator / denominator).astype(jnp.bfloat16)
    head_out = jnp.einsum(
        "hgqk,khd->qhgd", weights, blocked_values, preferred_element_type=jnp.float32
    )
    head_out = head_out.astype(jnp.bfloat16).reshape(tok_count, q_heads * HEAD_SIZE)
    gathered = lax.all_gather(head_out, "tp", axis=1, tiled=True)
    attended = jnp.dot(
        gathered,
        lax.all_gather(w_out, "seq", axis=0, tiled=True),
        preferred_element_type=jnp.float32,
    )
    stream = residual.astype(jnp.float32) + attended
    squares = lax.psum(jnp.sum(stream * stream, axis=1), "tp")
    normed = (stream * lax.rsqrt(squares / D + EPSILON)[:, None] * norm_gain[None, :]).astype(
        jnp.bfloat16
    )
    seq_count = lax.axis_size("seq")
    experts = seq_count // 2
    capacity = 2 * ((5 * tok_count * TOP + 8 * experts - 1) // (8 * experts))
    present = expert_ids[:, :, None] == jnp.arange(experts, dtype=jnp.int32)[None, None, :]
    per_row = jnp.sum(present.astype(jnp.int32), axis=1)
    before = jnp.cumsum(per_row, axis=0) - per_row
    position = jnp.sum(jnp.where(present, before[:, None, :], 0), axis=2)
    halves = jnp.arange(2, dtype=jnp.int32)
    targets = (2 * expert_ids[:, :, None] + halves[None, None, :]) * capacity + position[:, :, None]
    slot_count = seq_count * capacity
    slot_ids = jnp.arange(slot_count, dtype=jnp.int32)
    quarter = normed.shape[1]
    matches = (slot_ids[:, None, None, None] == targets[None]).astype(jnp.bfloat16)
    routing = jnp.sum(matches, axis=(2, 3))
    sending = jnp.dot(routing, normed, preferred_element_type=jnp.float32).astype(jnp.bfloat16)
    arrived = lax.all_to_all(
        sending.reshape(seq_count, capacity, quarter),
        "seq",
        split_axis=0,
        concat_axis=0,
        tiled=True,
    )
    expert_rows = arrived.reshape(slot_count, quarter)
    gate_part = jnp.dot(expert_rows, w_gate, preferred_element_type=jnp.float32)
    up_part = jnp.dot(expert_rows, w_up, preferred_element_type=jnp.float32)
    gate_sum, up_sum = (
        lax.psum_scatter(
            gate_part.astype(jnp.bfloat16), "tp", scatter_dimension=1, tiled=True
        ).astype(jnp.float32),
        lax.psum_scatter(
            up_part.astype(jnp.bfloat16), "tp", scatter_dimension=1, tiled=True
        ).astype(jnp.float32),
    )
    active = (jax.nn.silu(gate_sum) * up_sum).astype(jnp.bfloat16)
    produced = jnp.dot(
        lax.all_gather(active, "tp", axis=1, tiled=True), w_down, preferred_element_type=jnp.float32
    )
    produced = produced.astype(jnp.bfloat16).reshape(seq_count, capacity, quarter)
    returned = lax.all_to_all(produced, "seq", split_axis=0, concat_axis=0, tiled=True)
    both = returned.reshape(experts, 2, capacity, quarter)
    paired = (both[:, 0].astype(jnp.float32) + both[:, 1].astype(jnp.float32)).astype(jnp.bfloat16)
    paired = paired.reshape(experts * capacity, quarter)
    pair_slot = expert_ids * capacity + position
    pair_ids = jnp.arange(experts * capacity, dtype=jnp.int32)
    mixing = jnp.where(
        pair_ids[None, :, None] == pair_slot[:, None, :],
        expert_gates[:, None, :],
        jnp.zeros((), jnp.bfloat16),
    )
    mixing = jnp.sum(mixing, axis=2)
    blended = jnp.dot(mixing, paired, preferred_element_type=jnp.float32)
    return (stream + blended).astype(jnp.bfloat16)


def solution(mesh):
    return jax.shard_map(
        shards,
        mesh=mesh,
        in_specs=(
            P("seq", "tp"),
            P("seq", "tp"),
            P("seq", "tp"),
            P("tp"),
            P("seq"),
            P("seq", "tp"),
            P("seq", "tp"),
            P("tp"),
            P("seq", None),
            P("seq", None),
            P("tp", "seq"),
            P("tp", "seq"),
            P("seq", "tp"),
        ),
        out_specs=P("seq", "tp"),
        check_vma=False,
    )
```

profile of v0, /device:TPU:72, one launch (start us, length us, event | category | flops | bytes accessed | tf_op | source)
XLA Modules:
  0.0 459.0 jit_solution(16349413189414434142)
XLA Ops:
  6.5 0.0 copy-start
  6.5 0.0 all-gather.5.cloned.1.call-start
  6.5 2.0 collective-permute-start.1
  8.6 4.4 collective-permute-start
  13.0 1.4 fusion.18
  14.4 1.1 copy.51
  15.6 0.7 max.18
  16.3 0.0 collective-permute-done.1
  16.3 0.8 pad_maximum_fusion.1
  17.1 0.7 copy.50
  17.8 1.4 fusion.4
  19.2 0.0 copy-start.2
  19.2 0.1 broadcast_maximum_fusion
  19.3 0.0 copy-done.1
  19.3 0.5 fusion.5
  19.8 0.1 exponential_add_fusion
  19.8 0.0 collective-permute-done
  19.8 0.0 copy-done.3
  19.9 0.1 copy.49
  20.0 0.1 copy-done.2
  20.1 1.4 convolution_convert_fusion.4
  21.5 0.0 all-gather.5.cloned.1.call-update
  21.5 0.0 all-gather.7.cloned.1.call-start
  21.6 0.7 all-gather.7.cloned.1.call-update
  22.3 0.0 all-gather.9.cloned.1.call-start
  22.3 0.1 copy.53
  22.4 0.2 reduce_window_sum.11
  22.6 0.1 copy.55
  22.8 0.7 fusion.3
  23.4 0.0 copy-start.5
  23.4 30.5 %all-gather.5.cloned.1.call-done = bf16[128,4096]{0,1:T(8,128)(2,1)} async-done(((bf16[128,1024]{0,1:T(8,128)(2,1)}), bf16[128,4096]{0,1:T(8,128)(2,1)}) %all-gather.5.cloned.1.call-update) | async-done | bytes 1048592 | tf_op jit(solution)/shard_map/all_gather | solution.py:67
  53.9 88.6 %all-gather.7.cloned.1.call-done = bf16[4096,720]{1,0:T(8,128)(2,1)} async-done(((bf16[32,720]{1,0:T(8,128)(2,1)}), bf16[4096,720]{1,0:T(8,128)(2,1)}) %all-gather.7.cloned.1.call-update) | async-done | bytes 5898256 | tf_op jit(solution)/shard_map/all_gather | solution.py:70
  142.5 5.1 %multiply_reduce_fusion = (f32[128]{0:T(128)S(1)}, f32[128,720]{0,1:T(8,128)S(1)}) fusion(bf16[128,4096]{0,1:T(8,128)(2,1)} %all-gather.5.cloned.1.call-done, bf16[4096,720]{1,0:T(8,128)(2,1)} %all-gather.7.cloned.1.call-done, bf16[128,720]{0,1:T(8,128)(2,1)} %param.18), kind=kOutput, calls=%fused_computation.31 | convolution fusion | flops 755343232 | bytes 7500288 | tf_op jit(solution)/shard_map/dot_general | solution.py:68
  147.6 10.4 %psum.7 = f32[128]{0:T(128)S(1)} all-reduce(f32[128]{0:T(128)S(1)} %get-tuple-element.15), channel_id=1, replica_groups=mesh['seq'=128,'tp'=4] {'tp'}, use_global_device_ids=true, to_apply=%region_8.9 | all-reduce | flops 128 | bytes 1024 | tf_op jit(solution)/shard_map/psum | solution.py:74
  158.0 2.0 convolution_convert_fusion
  160.0 2.6 copy.56
  162.6 2.5 reshape.190
  165.1 86.3 %all_to_all.10 = bf16[128,10,720]{2,1,0:T(8,128)(2,1)} all-to-all(bf16[128,10,720]{2,1,0:T(8,128)(2,1)} %reshape.190), channel_id=1, replica_groups=mesh['seq'=128,'tp'=4] {'seq'}, dimensions={0} | all-to-all | bytes 3686400 | tf_op jit(solution)/shard_map/all_to_all | solution.py:93
  251.4 3.9 reshape.191
  255.4 0.0 copy-start.7
  255.4 3.0 convolution_convert_fusion.2
  258.4 2.9 convolution_convert_fusion.3
  261.3 46.3 %fusion.22 = (bf16[1280,184]{0,1:T(8,128)(2,1)S(1)}, bf16[1280,184]{0,1:T(8,128)(2,1)S(1)}) fusion(bf16[1280,720]{0,1:T(8,128)(2,1)} %convolution_convert_fusion.2, bf16[1280,720]{0,1:T(8,128)(2,1)} %convolution_convert_fusion.3), kind=kCustom, calls=%all-reduce-scatter.2 | all-reduce-scatter fusion | flops 1884161 | bytes 4630528
  307.7 1.3 collective-permute-start.2
  309.0 3.3 collective-permute-start.3
  312.3 1.3 dynamic-slice.6
  314.2 0.0 collective-permute-done.2
  314.3 0.6 concatenate.8
  314.9 0.0 collective-permute-done.3
  314.9 0.6 concatenate.9
  315.6 1.2 fusion.14
  316.7 0.0 all-gather.9.cloned.1.call-update
  316.8 29.1 %all-gather.9.cloned.1.call-done = bf16[4,180,1280]{2,1,0:T(8,128)(2,1)} async-done(((bf16[1,180,1280]{2,1,0:T(8,128)(2,1)}), bf16[4,180,1280]{2,1,0:T(8,128)(2,1)}) %all-gather.9.cloned.1.call-update) | async-done | bytes 1843216 | tf_op jit(solution)/shard_map/all_gather | solution.py:113
  345.9 1.7 reshape.195
  347.5 4.2 convolution_convert_fusion.1
  351.8 2.6 copy.57
  354.4 2.5 reshape.192
  356.9 14.5 %all-to-all-start.1 = ((bf16[128,10,720]{2,1,0:T(8,128)(2,1)}), bf16[128,10,720]{2,1,0:T(8,128)(2,1)}, u32[]{:S(2)}, u32[]{:S(2)}) async-start(bf16[128,10,720]{2,1,0:T(8,128)(2,1)} %reshape.192), calls=%async_computation.1 | async-start | bytes 6291456 | tf_op jit(solution)/shard_map/all_to_all | solution.py:116
  371.4 0.0 copy-done.6
  371.4 0.2 fusion.13
  371.7 74.7 %all-to-all-done.1 = bf16[128,10,720]{2,1,0:T(8,128)(2,1)} async-done(((bf16[128,10,720]{2,1,0:T(8,128)(2,1)}), bf16[128,10,720]{2,1,0:T(8,128)(2,1)}, u32[]{:S(2)}, u32[]{:S(2)}) %all-to-all-start.1) | async-done | bytes 1843232 | tf_op jit(solution)/shard_map/all_to_all | solution.py:116
  446.4 2.3 add_convert_fusion
  448.7 1.4 convert_element_type.92
  450.1 2.4 fusion.7
  (19 shorter events, 0.2 us)
Async XLA Ops:
  6.5 248.8 %copy-start = (bf16[720,720]{1,0:T(8,128)(2,1)S(1)}, bf16[720,720]{1,0:T(8,128)(2,1)}, u32[]{:S(2)}) copy-start(bf16[720,720]{1,0:T(8,128)(2,1)} %param.24) | copy-start | bytes 3110404
  6.5 47.4 %all-gather.5.cloned.1.call-start = ((), (), s32[]{:S(2)}) async-start(), calls=%async_computation.2 | async-start | bytes 1310720 | tf_op jit(solution)/shard_map/all_gather | solution.py:67
  6.5 9.8 %collective-permute-start.1 = (bf16[128,128]{1,0:T(8,128)(2,1)}, bf16[128,128]{1,0:T(8,128)(2,1)S(1)}, u32[]{:S(2)}, u32[]{:S(2)}) collective-permute-start(bf16[128,128]{1,0:T(8,128)(2,1)} %param.14), channel_id=1, source_target_pairs={{0,4},{4,8},{8,12},{12,16},{16,20},{20,24},{24,28},{28,32},{32,36}... | collective-permute-start | bytes 98312 | tf_op jit(solution)/shard_map/ppermute | solution.py:17
  8.6 11.3 %collective-permute-start = (bf16[128,128]{1,0:T(8,128)(2,1)}, bf16[128,128]{1,0:T(8,128)(2,1)S(1)}, u32[]{:S(2)}, u32[]{:S(2)}) collective-permute-start(bf16[128,128]{1,0:T(8,128)(2,1)} %param.15), channel_id=1, source_target_pairs={{0,4},{4,8},{8,12},{12,16},{16,20},{20,24},{24,28},{28,32},{32,36}... | collective-permute-start | bytes 98312 | tf_op jit(solution)/shard_map/ppermute | solution.py:17
  17.8 1.5 copy-start.1
  17.8 2.0 copy-start.3
  19.2 0.9 copy-start.2
  20.1 2.2 copy-start.4
  21.5 121.0 %all-gather.7.cloned.1.call-start = ((), (), s32[]{:S(2)}) async-start(), calls=%async_computation.3 | async-start | bytes 6340608 | tf_op jit(solution)/shard_map/all_gather | solution.py:70
  22.3 323.6 %all-gather.9.cloned.1.call-start = ((), (), s32[]{:S(2)}) async-start(), calls=%async_computation.4 | async-start | bytes 2355200 | tf_op jit(solution)/shard_map/all_gather | solution.py:113
  23.4 134.6 %copy-start.5 = (f32[720]{0:T(1024)S(1)}, f32[720]{0:T(1024)}, u32[]{:S(2)}) copy-start(f32[720]{0:T(1024)} %param.20) | copy-start | bytes 8644
  255.4 3.0 copy-start.7
  307.7 6.6 %collective-permute-start.2 = (bf16[1280,12]{0,1:T(8,128)(2,1)S(1)}, bf16[1280,12]{0,1:T(8,128)(2,1)S(1)}, u32[]{:S(2)}, u32[]{:S(2)}) collective-permute-start(bf16[1280,12]{0,1:T(8,128)(2,1)S(1)} %slice.10), channel_id=1, source_target_pairs={{0,1},{1,2},{2,3},{4,5},{5,6},{6,7},{8,9},{9,10},{10,11},{12,13},{... | collective-permute-start | bytes 92168
  309.0 5.9 %collective-permute-start.3 = (bf16[1280,12]{0,1:T(8,128)(2,1)S(1)}, bf16[1280,12]{0,1:T(8,128)(2,1)S(1)}, u32[]{:S(2)}, u32[]{:S(2)}) collective-permute-start(bf16[1280,12]{0,1:T(8,128)(2,1)S(1)} %slice.11), channel_id=1, source_target_pairs={{0,1},{1,2},{2,3},{4,5},{5,6},{6,7},{8,9},{9,10},{10,11},{12,13},{... | collective-permute-start | bytes 92168
  356.9 14.5 %copy-start.6 = (bf16[128,4]{0,1:T(4,128)(2,1)S(1)}, bf16[128,4]{0,1:T(4,128)(2,1)}, u32[]{:S(2)}) copy-start(bf16[128,4]{0,1:T(4,128)(2,1)} %param.22) | copy-start | bytes 3076
  356.9 89.5 %all-to-all-start.1 = ((bf16[128,10,720]{2,1,0:T(8,128)(2,1)}), bf16[128,10,720]{2,1,0:T(8,128)(2,1)}, u32[]{:S(2)}, u32[]{:S(2)}) async-start(bf16[128,10,720]{2,1,0:T(8,128)(2,1)} %reshape.192), calls=%async_computation.1 | async-start | bytes 6291456 | tf_op jit(solution)/shard_map/all_to_all | solution.py:116
Sparse Core Ops, SparseCore 0:
  21.6 32.2 all-gather.4
  57.0 85.4 all-gather.6
  316.9 28.9 all-gather.8
where the time goes:
time: 460 us; the launch traced here: 459 us
  waiting for transfers between devices  224 us (49%)
  blocking collectives  143 us (31%)
  starting transfers between devices  25.6 us (6%)
  local copies, waits for them, and re-layouts  22.8 us (5%)
  matrix products  22.4 us (5%)
  between operations  14.1 us (3%)
  other arithmetic  7.47 us (2%)
    all_gather x1, waiting for transfers between devices, shards(): lax.all_gather(w_out, 'seq', axis=0, tiled=True)  88.6 us
    all_to_all x1, blocking collectives, shards(): lax.all_to_all(sending.reshape(seq_count, capacity, quarter), 'seq', spli...  86.3 us
    all_to_all x1, waiting for transfers between devices, shards(): lax.all_to_all(produced, 'seq', split_axis=0, concat_axis=0, tiled=True)  74.7 us
    unnamed x1, blocking collectives  46.3 us
    all_gather x1, waiting for transfers between devices, shards(): gathered = lax.all_gather(head_out, 'tp', axis=1, tiled=True)  30.5 us
    all_gather x1, waiting for transfers between devices, shards(): lax.all_gather(active, 'tp', axis=1, tiled=True)  29.1 us
    all_to_all x1, starting transfers between devices, shards(): lax.all_to_all(produced, 'seq', split_axis=0, concat_axis=0, tiled=True)  14.5 us
    psum x1, blocking collectives, shards(): squares = lax.psum(jnp.sum(stream * stream, axis=1), 'tp')  10.4 us
  transfers between devices with their start and end apart: 8, of which 4 were waited for; matrix products, arithmetic and copies ran while one was open for 2% of the time, Pallas kernels for 0%

commit v1 on v0

--- a/solution.py
+++ b/solution.py
@@ -64,7 +64,9 @@
         "hgqk,khd->qhgd", weights, blocked_values, preferred_element_type=jnp.float32
     )
     head_out = head_out.astype(jnp.bfloat16).reshape(tok_count, q_heads * HEAD_SIZE)
-    gathered = lax.all_gather(head_out, "tp", axis=1, tiled=True)
+    gathered = jnp.concatenate(
+        lax.all_to_all(jnp.stack([head_out] * lax.axis_size("tp")), "tp", 0, 0), axis=1
+    )
     attended = jnp.dot(
         gathered,
         lax.all_gather(w_out, "seq", axis=0, tiled=True),

time: 460 us -> 417 us (0.907)
  waiting for transfers between devices: 224 us -> 177 us
    all_gather x1 -> x0, waiting for transfers between devices: 30.5 us -> none  [shards(): gathered = lax.all_gather(head_out, 'tp', axis=1, tiled=True)]
    all_gather x1, waiting for transfers between devices: 88.6 us -> 58.8 us  [shards(): lax.all_gather(w_out, 'seq', axis=0, tiled=True)]
    all_to_all x0 -> x1, waiting for transfers between devices: none -> 14.2 us  [shards(): lax.all_to_all(jnp.stack([head_out] * lax.axis_size('tp')), 'tp', 0, 0)]
  transfers between devices with their start and end apart: 8 -> 8, of which waited for: 4 -> 4; matrix products, arithmetic and copies ran while one was open for 2% -> 3% of each run, Pallas kernels for 0% -> 0%
where the time goes in v1:
time: 417 us; the launch traced here: 416 us
  waiting for transfers between devices  177 us (42%)
  blocking collectives  143 us (34%)
  starting transfers between devices  29.7 us (7%)
  local copies, waits for them, and re-layouts  23.2 us (6%)
  matrix products  20.6 us (5%)
  between operations  14.3 us (3%)
  other arithmetic  7.58 us (2%)
    all_to_all x1, blocking collectives, shards(): lax.all_to_all(sending.reshape(seq_count, capacity, quarter), 'seq', spli...  86.3 us
    all_to_all x1, waiting for transfers between devices, shards(): lax.all_to_all(produced, 'seq', split_axis=0, concat_axis=0, tiled=True)  74.7 us
    all_gather x1, waiting for transfers between devices, shards(): lax.all_gather(w_out, 'seq', axis=0, tiled=True)  58.8 us
    unnamed x1, blocking collectives  46.3 us
    all_gather x1, waiting for transfers between devices, shards(): lax.all_gather(active, 'tp', axis=1, tiled=True)  29.1 us
    all_to_all x1, starting transfers between devices, shards(): lax.all_to_all(produced, 'seq', split_axis=0, concat_axis=0, tiled=True)  14.5 us
    all_to_all x1, waiting for transfers between devices, shards(): lax.all_to_all(jnp.stack([head_out] * lax.axis_size('tp')), 'tp', 0, 0)  14.2 us
    psum x1, blocking collectives, shards(): squares = lax.psum(jnp.sum(stream * stream, axis=1), 'tp')  10.4 us
  transfers between devices with their start and end apart: 8, of which 4 were waited for; matrix products, arithmetic and copies ran while one was open for 3% of the time, Pallas kernels for 0%

profile of v1, /device:TPU:72, one launch (start us, length us, event | category | flops | bytes accessed | tf_op | source)
XLA Modules:
  0.0 416.0 jit_solution(3368298067839414780)
XLA Ops:
  6.5 0.0 copy-start
  6.5 0.0 all-gather.4.cloned.1.call-start
  6.5 0.7 all-gather.4.cloned.1.call-update
  7.3 1.9 collective-permute-start.1
  9.2 4.4 %collective-permute-start = (bf16[128,128]{1,0:T(8,128)(2,1)}, bf16[128,128]{1,0:T(8,128)(2,1)S(1)}, u32[]{:S(2)}, u32[]{:S(2)}) collective-permute-start(bf16[128,128]{1,0:T(8,128)(2,1)} %param.15), channel_id=1, source_target_pairs={{0,4},{4,8},{8,12},{12,16},{16,20},{20,24},{24,28},{28,32},{32,36}... | collective-permute-start | bytes 98312 | tf_op jit(solution)/shard_map/ppermute | solution.py:17
  13.6 0.8 fusion.18
  14.4 1.1 copy.52
  15.5 0.7 max.18
  16.3 0.0 collective-permute-done.1
  16.3 0.8 pad_maximum_fusion.1
  17.0 0.1 copy.51
  17.1 0.0 collective-permute-done
  17.1 0.8 pad_maximum_fusion
  17.9 0.1 copy.50
  18.0 0.5 fusion.4
  18.5 0.1 broadcast_maximum_fusion
  18.6 0.5 fusion.5
  19.1 0.1 exponential_add_fusion
  19.2 0.7 convolution_convert_fusion.4
  19.9 0.0 copy-start.1
  19.9 1.1 stack.3
  21.1 4.3 %all-to-all-start = ((bf16[4,128,1024]{1,2,0:T(8,128)(2,1)}), bf16[4,128,1024]{1,2,0:T(8,128)(2,1)S(1)}, u32[]{:S(2)}, u32[]{:S(2)}) async-start(bf16[4,128,1024]{1,2,0:T(8,128)(2,1)} %stack.3), calls=%async_computation | async-start | bytes 2097152 | tf_op jit(solution)/shard_map/all_to_all | solution.py:68
  25.4 0.0 all-gather.6.cloned.1.call-start
  25.4 0.0 copy-done.2
  25.4 0.1 copy.54
  25.5 0.2 reduce_window_sum.11
  25.7 0.1 copy.56
  25.8 0.7 fusion.3
  26.5 14.2 %all-to-all-done = bf16[4,128,1024]{1,2,0:T(8,128)(2,1)S(1)} async-done(((bf16[4,128,1024]{1,2,0:T(8,128)(2,1)}), bf16[4,128,1024]{1,2,0:T(8,128)(2,1)S(1)}, u32[]{:S(2)}, u32[]{:S(2)}) %all-to-all-start) | async-done | bytes 1048608 | tf_op jit(solution)/shard_map/all_to_all | solution.py:68
  40.6 58.8 %all-gather.4.cloned.1.call-done = bf16[4096,720]{1,0:T(8,128)(2,1)} async-done(((bf16[32,720]{1,0:T(8,128)(2,1)}), bf16[4096,720]{1,0:T(8,128)(2,1)}) %all-gather.4.cloned.1.call-update) | async-done | bytes 5898256 | tf_op jit(solution)/shard_map/all_gather | solution.py:72
  99.4 0.0 copy-done.1
  99.4 4.9 %multiply_reduce_fusion = (f32[128]{0:T(128)S(1)}, f32[128,720]{0,1:T(8,128)S(1)}) fusion(bf16[128,4096]{0,1:T(8,128)(2,1)S(1)} %bitcast.63, bf16[4096,720]{1,0:T(8,128)(2,1)} %all-gather.4.cloned.1.call-done, bf16[128,720]{0,1:T(8,128)(2,1)S(1)} %copy-done.1), kind=kOutput, calls=%fused_computation.31 | convolution fusion | flops 755343232 | bytes 7500288 | tf_op jit(solution)/shard_map/dot_general | solution.py:70
  104.3 10.4 %psum.7 = f32[128]{0:T(128)S(1)} all-reduce(f32[128]{0:T(128)S(1)} %get-tuple-element.15), channel_id=1, replica_groups=mesh['seq'=128,'tp'=4] {'tp'}, use_global_device_ids=true, to_apply=%region_8.9 | all-reduce | flops 128 | bytes 1024 | tf_op jit(solution)/shard_map/psum | solution.py:76
  114.7 0.0 copy-done.3
  114.7 2.0 convolution_convert_fusion
  116.7 2.6 copy.57
  119.3 2.5 reshape.196
  121.8 86.3 %all_to_all.15 = bf16[128,10,720]{2,1,0:T(8,128)(2,1)} all-to-all(bf16[128,10,720]{2,1,0:T(8,128)(2,1)} %reshape.196), channel_id=1, replica_groups=mesh['seq'=128,'tp'=4] {'seq'}, dimensions={0} | all-to-all | bytes 3686400 | tf_op jit(solution)/shard_map/all_to_all | solution.py:95
  208.1 3.9 reshape.197
  212.1 0.0 copy-start.5
  212.1 3.0 convolution_convert_fusion.2
  215.1 2.9 convolution_convert_fusion.3
  218.0 46.3 %fusion.22 = (bf16[1280,184]{0,1:T(8,128)(2,1)S(1)}, bf16[1280,184]{0,1:T(8,128)(2,1)S(1)}) fusion(bf16[1280,720]{0,1:T(8,128)(2,1)} %convolution_convert_fusion.2, bf16[1280,720]{0,1:T(8,128)(2,1)} %convolution_convert_fusion.3), kind=kCustom, calls=%all-reduce-scatter.2 | all-reduce-scatter fusion | flops 1884161 | bytes 4630528
  264.4 1.3 collective-permute-start.2
  265.7 3.3 collective-permute-start.3
  269.0 1.3 dynamic-slice.6
  271.0 0.0 collective-permute-done.2
  271.0 0.6 concatenate.8
  271.6 0.0 collective-permute-done.3
  271.6 0.6 concatenate.9
  272.3 1.2 fusion.14
  273.4 0.0 all-gather.6.cloned.1.call-update
  273.5 29.1 %all-gather.6.cloned.1.call-done = bf16[4,180,1280]{2,1,0:T(8,128)(2,1)} async-done(((bf16[1,180,1280]{2,1,0:T(8,128)(2,1)}), bf16[4,180,1280]{2,1,0:T(8,128)(2,1)}) %all-gather.6.cloned.1.call-update) | async-done | bytes 1843216 | tf_op jit(solution)/shard_map/all_gather | solution.py:115
  302.6 1.7 reshape.201
  304.2 4.2 %convolution_convert_fusion.1 = bf16[1280,720]{0,1:T(8,128)(2,1)} fusion(bf16[720,1280]{1,0:T(8,128)(2,1)S(1)} %reshape.201, bf16[720,720]{1,0:T(8,128)(2,1)} %param.25), kind=kOutput, calls=%fused_computation.3 | convolution fusion | flops 1328025600 | bytes 4723200 | tf_op jit(solution)/shard_map/dot_general | solution.py:114
  308.5 2.6 copy.58
  311.1 2.5 reshape.198
  313.6 14.5 %all-to-all-start.2 = ((bf16[128,10,720]{2,1,0:T(8,128)(2,1)}), bf16[128,10,720]{2,1,0:T(8,128)(2,1)}, u32[]{:S(2)}, u32[]{:S(2)}) async-start(bf16[128,10,720]{2,1,0:T(8,128)(2,1)} %reshape.198), calls=%async_computation.2 | async-start | bytes 6291456 | tf_op jit(solution)/shard_map/all_to_all | solution.py:118
  328.1 0.0 copy-done.4
  328.1 0.2 fusion.13
  328.4 74.7 %all-to-all-done.2 = bf16[128,10,720]{2,1,0:T(8,128)(2,1)} async-done(((bf16[128,10,720]{2,1,0:T(8,128)(2,1)}), bf16[128,10,720]{2,1,0:T(8,128)(2,1)}, u32[]{:S(2)}, u32[]{:S(2)}) %all-to-all-start.2) | async-done | bytes 1843232 | tf_op jit(solution)/shard_map/all_to_all | solution.py:118
  403.1 2.3 add_convert_fusion
  405.4 1.4 convert_element_type.92
  406.8 2.4 fusion.7
  (15 shorter events, 0.1 us)
Async XLA Ops:
  6.5 205.5 %copy-start = (bf16[720,720]{1,0:T(8,128)(2,1)S(1)}, bf16[720,720]{1,0:T(8,128)(2,1)}, u32[]{:S(2)}) copy-start(bf16[720,720]{1,0:T(8,128)(2,1)} %param.24) | copy-start | bytes 3110404
  6.5 92.9 %all-gather.4.cloned.1.call-start = ((), (), s32[]{:S(2)}) async-start(), calls=%async_computation.3 | async-start | bytes 6340608 | tf_op jit(solution)/shard_map/all_gather | solution.py:72
  7.3 9.0 %collective-permute-start.1 = (bf16[128,128]{1,0:T(8,128)(2,1)}, bf16[128,128]{1,0:T(8,128)(2,1)S(1)}, u32[]{:S(2)}, u32[]{:S(2)}) collective-permute-start(bf16[128,128]{1,0:T(8,128)(2,1)} %param.14), channel_id=1, source_target_pairs={{0,4},{4,8},{8,12},{12,16},{16,20},{20,24},{24,28},{28,32},{32,36}... | collective-permute-start | bytes 98312 | tf_op jit(solution)/shard_map/ppermute | solution.py:17
  9.2 7.9 %collective-permute-start = (bf16[128,128]{1,0:T(8,128)(2,1)}, bf16[128,128]{1,0:T(8,128)(2,1)S(1)}, u32[]{:S(2)}, u32[]{:S(2)}) collective-permute-start(bf16[128,128]{1,0:T(8,128)(2,1)} %param.15), channel_id=1, source_target_pairs={{0,4},{4,8},{8,12},{12,16},{16,20},{20,24},{24,28},{28,32},{32,36}... | collective-permute-start | bytes 98312 | tf_op jit(solution)/shard_map/ppermute | solution.py:17
  19.9 5.5 %copy-start.2 = (s32[128,4]{0,1:T(4,128)S(1)}, s32[128,4]{0,1:T(4,128)}, u32[]{:S(2)}) copy-start(s32[128,4]{0,1:T(4,128)} %param.21) | copy-start | bytes 6148
  19.9 79.5 %copy-start.1 = (bf16[128,720]{0,1:T(8,128)(2,1)S(1)}, bf16[128,720]{0,1:T(8,128)(2,1)}, u32[]{:S(2)}) copy-start(bf16[128,720]{0,1:T(8,128)(2,1)} %param.18) | copy-start | bytes 552964
  21.1 19.6 %all-to-all-start = ((bf16[4,128,1024]{1,2,0:T(8,128)(2,1)}), bf16[4,128,1024]{1,2,0:T(8,128)(2,1)S(1)}, u32[]{:S(2)}, u32[]{:S(2)}) async-start(bf16[4,128,1024]{1,2,0:T(8,128)(2,1)} %stack.3), calls=%async_computation | async-start | bytes 2097152 | tf_op jit(solution)/shard_map/all_to_all | solution.py:68
  25.4 277.2 %all-gather.6.cloned.1.call-start = ((), (), s32[]{:S(2)}) async-start(), calls=%async_computation.4 | async-start | bytes 2355200 | tf_op jit(solution)/shard_map/all_gather | solution.py:115
  99.4 15.3 %copy-start.3 = (f32[720]{0:T(1024)S(1)}, f32[720]{0:T(1024)}, u32[]{:S(2)}) copy-start(f32[720]{0:T(1024)} %param.20) | copy-start | bytes 8644
  212.1 3.0 copy-start.5
  264.4 6.6 %collective-permute-start.2 = (bf16[1280,12]{0,1:T(8,128)(2,1)S(1)}, bf16[1280,12]{0,1:T(8,128)(2,1)S(1)}, u32[]{:S(2)}, u32[]{:S(2)}) collective-permute-start(bf16[1280,12]{0,1:T(8,128)(2,1)S(1)} %slice.10), channel_id=1, source_target_pairs={{0,1},{1,2},{2,3},{4,5},{5,6},{6,7},{8,9},{9,10},{10,11},{12,13},{... | collective-permute-start | bytes 92168
  265.7 5.9 %collective-permute-start.3 = (bf16[1280,12]{0,1:T(8,128)(2,1)S(1)}, bf16[1280,12]{0,1:T(8,128)(2,1)S(1)}, u32[]{:S(2)}, u32[]{:S(2)}) collective-permute-start(bf16[1280,12]{0,1:T(8,128)(2,1)S(1)} %slice.11), channel_id=1, source_target_pairs={{0,1},{1,2},{2,3},{4,5},{5,6},{6,7},{8,9},{9,10},{10,11},{12,13},{... | collective-permute-start | bytes 92168
  313.6 14.5 %copy-start.4 = (bf16[128,4]{0,1:T(4,128)(2,1)S(1)}, bf16[128,4]{0,1:T(4,128)(2,1)}, u32[]{:S(2)}) copy-start(bf16[128,4]{0,1:T(4,128)(2,1)} %param.22) | copy-start | bytes 3076
  313.6 89.5 %all-to-all-start.2 = ((bf16[128,10,720]{2,1,0:T(8,128)(2,1)}), bf16[128,10,720]{2,1,0:T(8,128)(2,1)}, u32[]{:S(2)}, u32[]{:S(2)}) async-start(bf16[128,10,720]{2,1,0:T(8,128)(2,1)} %reshape.198), calls=%async_computation.2 | async-start | bytes 6291456 | tf_op jit(solution)/shard_map/all_to_all | solution.py:118
Sparse Core Ops, SparseCore 0:
  10.5 88.8 all-gather.3
  273.6 28.9 all-gather.5
